TPU v7x, 256 devices: a whole 4x4x8 slice. The times are simulated.
256 devices in a mesh: pair: 64 (over y, z, core), red: 4 (over x).
Axes of the slice: x: 4, y: 4, z: 8, core: 2. Of those that a mesh axis runs over, the one named last changes fastest.
Arguments:
- amplitudes: bfloat16 [64, 64, 8192], P('pair', None, 'red'), may hold values from -6 to 6
- integrals: bfloat16 [8192, 8192], P('red'), may hold values from -0.1875 to 0.1875
- occ_irrep: int32 [64], replicated, may hold values from 0 to 7
- vir_irrep: int32 [512], replicated, may hold values from 0 to 7, as said below
- cd_orbitals: int32 [2, 8192], P(None, 'red'), may hold values from 0 to 511
- ab_orbitals: int32 [2, 8192], P(None, 'pair'), may hold values from 0 to 511, as said below
Outputs:
- residual: bfloat16 [64, 64, 8192], P(None, 'red', 'pair')
Inputs may be any that keep to these rules, and one draw needn't show every extreme that they name: `vir_irrep`: D2h irrep labels; each label is held by exactly 64 virtual orbitals. `occ_irrep`: D2h irrep labels. `cd_orbitals`: indices of virtual orbitals. `ab_orbitals`: indices of virtual orbitals; the slab pairs m with m // 128 equal come as 8 blocks of 16 pairs, and ab_irrep[m] = (m % 128) // 16.
All inputs are finite; a program needn't handle non-finite values.
Results may differ from a plain program's by a relative error of at most 0.001.
Values may be sent and summed in bfloat16 or wider, within the bound.
A program may use at most 192 MiB of HBM per device.

v0:
```python
import jax
import jax.numpy as jnp
from jax import lax
from jax.sharding import PartitionSpec as P


def pair_labels(orbitals, vir_irrep):
    labels = lax.broadcasted_iota(jnp.int32, (1, vir_irrep.shape[0]), 1)
    first_label = jnp.sum(jnp.where(orbitals[0][:, None] == labels, vir_irrep[None, :], 0), axis=1)
    second_label = jnp.sum(jnp.where(orbitals[1][:, None] == labels, vir_irrep[None, :], 0), axis=1)
    return jnp.bitwise_xor(first_label, second_label)


def local(amplitudes, integrals, occ_irrep, vir_irrep, cd_orbitals, ab_orbitals):
    own_rows = amplitudes.shape[0]
    occupied = amplitudes.shape[1]
    slab_width = integrals.shape[1]
    first_row = lax.axis_index("pair") * own_rows
    own_irrep = lax.dynamic_slice_in_dim(occ_irrep, first_row, own_rows, 0)
    pair_irrep = jnp.bitwise_xor(own_irrep[:, None], occ_irrep[None, :])
    cd_irrep = pair_labels(cd_orbitals, vir_irrep)
    masked = jnp.where(
        pair_irrep[:, :, None] == cd_irrep[None, None, :],
        amplitudes,
        jnp.zeros((), amplitudes.dtype),
    )
    partial_sums = jnp.dot(
        masked.reshape(own_rows * occupied, masked.shape[2]),
        integrals,
        preferred_element_type=jnp.float32,
    )
    partial_sums = partial_sums.reshape(own_rows, occupied, slab_width)
    moved = lax.all_to_all(partial_sums, "pair", split_axis=2, concat_axis=0, tiled=True)
    summed = lax.psum_scatter(moved, "red", scatter_dimension=1, tiled=True)
    j_rows = summed.shape[1]
    j_irrep = lax.dynamic_slice_in_dim(occ_irrep, lax.axis_index("red") * j_rows, j_rows, 0)
    out_irrep = jnp.bitwise_xor(occ_irrep[:, None], j_irrep[None, :])
    ab_irrep = pair_labels(ab_orbitals, vir_irrep)
    kept = jnp.where(
        out_irrep[:, :, None] == ab_irrep[None, None, :], summed, jnp.zeros((), summed.dtype)
    )
    return kept.astype(jnp.bfloat16)


def solution(mesh):
    in_specs = (P("pair", None, "red"), P("red", None), P(), P(), P(None, "red"), P(None, "pair"))
    out_specs = P(None, "red", "pair")
    return jax.shard_map(local, mesh=mesh, in_specs=in_specs, out_specs=out_specs, check_vma=False)
```

profile of v0, /device:TPU:1, one launch (start us, length us, event | category | flops | bytes accessed | tf_op | source)
XLA Modules:
  0.0 194.9 jit_solution(4072649862004780560)
XLA Ops:
  6.5 0.0 reduce-scatter.2.cloned.1.call-start
  6.5 1.2 dynamic_slice.7
  7.8 1.3 broadcast_xor_fusion.1
  9.1 0.8 fusion.7
  9.9 2.3 %select_reduce_fusion = (s32[2048]{0:T(1024)S(1)}, s32[2048]{0:T(1024)S(1)}) fusion(s32[2048]{0:T(1024)S(1)} %bitcast.23, s32[512]{0:T(512)} %param.9, s32[2048]{0:T(1024)S(1)} %bitcast.22), kind=kLoop, calls=%fused_computation | loop fusion | flops 6287360 | bytes 34816 | tf_op jit(solution)/shard_map/reduce_sum | solution.py:10
  12.2 19.2 %fusion.1 = f32[64,8192]{0,1:T(8,128)} fusion(bf16[2048,8192]{1,0:T(8,128)(2,1)} %param.7, bf16[1,64,2048]{2,1,0:T(8,128)(2,1)} %param.6, s32[2048]{0:T(1024)S(1)} %xor.49, s32[64]{0:T(128)S(1)} %broadcast_xor_fusion.1), kind=kOutput, calls=%fused_computation.7 | convolution fusion | flops 2147745792 | bytes 35922176 | tf_op jit(solution)/shard_map/dot_general | solution.py:27
  31.4 0.5 broadcast.63
  32.0 38.4 %reduce = f32[8192,64]{1,0:T(8,128)} reduce(f32[8192,1,64]{2,1,0:T(1,128)} %bitcast.19, f32[]{:T(128)} %broadcast.63), dimensions={1}, to_apply=%bitcast.16.reduce_sub_computation | reduce | bytes 4194308
  70.4 4.6 %reshape.102 = f32[64,1,8192]{2,1,0:T(1,128)S(1)} reshape(f32[8192,64]{1,0:T(8,128)} %reduce) | data formatting | bytes 4194304
  74.9 64.3 %all_to_all.18 = f32[64,1,8192]{2,1,0:T(1,128)} all-to-all(f32[64,1,8192]{2,1,0:T(1,128)S(1)} %reshape.102), channel_id=1, replica_groups=mesh['pair'=64,'red'=4] {'pair'}, dimensions={0} | all-to-all | bytes 4194304 | tf_op jit(solution)/shard_map/all_to_all | solution.py:33
  139.2 7.5 %reduce.1 = f32[64,8192]{1,0:T(8,128)S(1)} reduce(f32[64,1,8192]{2,1,0:T(1,128)} %all_to_all.18, f32[]{:T(128)} %broadcast.63), dimensions={1}, to_apply=%all_to_all.13.reduce_sub_computation | reduce | bytes 4194308 | tf_op jit(solution)/shard_map/all_to_all | solution.py:33
  146.8 6.6 %reshape.103 = f32[8192,1,64]{2,1,0:T(1,128)} reshape(f32[64,8192]{1,0:T(8,128)S(1)} %reduce.1) | data formatting | bytes 4194304
  153.4 0.0 copy-start.2
  153.4 0.0 copy-start.1
  153.4 0.0 copy-start
  153.4 3.9 %copy.11 = f32[1,64,64,128]{3,1,2,0:T(8,128)} copy(f32[1,64,64,128]{1,3,2,0:T(8,128)} %bitcast.20) | data formatting | bytes 4194304 | tf_op jit(solution)/shard_map/all_to_all | solution.py:33
  157.2 0.0 reduce-scatter.2.cloned.1.call-update
  157.3 0.0 copy-done.2
  157.3 0.1 dynamic_slice.6
  157.3 0.0 copy-done.1
  157.3 0.0 copy-done
  157.4 0.2 select_reduce_fusion.2
  157.6 0.1 broadcast_xor_fusion
  157.6 28.5 %reduce-scatter.2.cloned.1.call-done = f32[64,16,128]{2,1,0:T(8,128)} async-done(((f32[64,64,128]{2,1,0:T(8,128)}), f32[64,16,128]{2,1,0:T(8,128)}) %reduce-scatter.2.cloned.1.call-update) | async-done | bytes 524304 | tf_op jit(solution)/shard_map/reduce_scatter | solution.py:34
  186.1 1.9 select_convert_fusion
  (3 shorter events, 0.0 us)
Async XLA Ops:
  6.5 179.6 %reduce-scatter.2.cloned.1.call-start = ((), (), s32[]{:S(2)}) async-start(), calls=%async_computation.2 | async-start | bytes 2621440 | tf_op jit(solution)/shard_map/reduce_scatter | solution.py:34
  153.4 3.9 %copy-start.2 = (s32[64]{0:T(128)S(1)}, s32[64]{0:T(128)}, u32[]{:S(2)}) copy-start(s32[64]{0:T(128)} %param.8) | copy-start | bytes 772
  153.4 4.0 %copy-start.1 = (s32[2,128]{1,0:T(2,128)S(1)}, s32[2,128]{1,0:T(2,128)}, u32[]{:S(2)}) copy-start(s32[2,128]{1,0:T(2,128)} %param.11) | copy-start | bytes 3076
  153.4 4.0 %copy-start = (s32[512]{0:T(512)S(1)}, s32[512]{0:T(512)}, u32[]{:S(2)}) copy-start(s32[512]{0:T(512)} %param.9) | copy-start | bytes 6148
Sparse Core Ops, SparseCore 0:
  157.4 28.6 reduce-scatter.1
where the time goes:
time: 195 us
  blocking collectives  64.3 us (33%)
  other arithmetic  51.8 us (27%)
  waiting for transfers between devices  28.5 us (15%)
  matrix products  19.2 us (10%)
  local copies, waits for them, and re-layouts  17.6 us (9%)
  between operations  13.5 us (7%)
    all_to_all x1, blocking collectives, local(): lax.all_to_all(partial_sums, 'pair', split_axis=2, concat_axis=0, tiled=T...  64.3 us
    unnamed x1, other arithmetic  38.4 us
    reduce_scatter x1, waiting for transfers between devices, local(): summed = lax.psum_scatter(moved, 'red', scatter_dimension=1, tiled=True)  28.5 us
    dot_general x1, matrix products, local(): jnp.dot(masked.reshape(own_rows * occupied, masked.shape[2]), integrals,...  19.2 us
    unnamed x9, local copies, waits for them, and re-layouts  11.6 us
    all_to_all x1, other arithmetic, local(): lax.all_to_all(partial_sums, 'pair', split_axis=2, concat_axis=0, tiled=T...  7.54 us
  transfers between devices with their start and end apart: 1, of which 1 were waited for; matrix products, arithmetic and copies ran while one was open for 0% of the time, Pallas kernels for 0%

commit v1 on v0

v1 whole, which is shorter than its diff:
```python
import functools

import jax
import jax.numpy as jnp
from jax import lax
from jax.experimental import pallas as pl
from jax.experimental.pallas import tpu as pltpu
from jax.sharding import PartitionSpec as P

NY, NZ = 4, 8
NC = NY * NZ
RED = 4
QG = 4
STEPS = NC // QG
LAG = 2
MESH = pl.DeviceIdType.MESH


def zigzag(t):
    half = lax.div(t + 1, 2)
    return half * (1 - 2 * lax.rem(t + 1, 2))


def chip_at(step, y, z):
    offset = NC - 1 - step
    dz = zigzag(lax.rem(offset, NZ))
    dy = zigzag(lax.div(offset, NZ))
    return lax.rem(y + dy + NY, NY) * NZ + lax.rem(z + dz + NZ, NZ)


def kernel(
    a_hbm, v_hbm, occ_hbm, vir_hbm, cd_hbm, o_hbm,
    vbuf, abuf, lhs, cdv, virv, occs, labels, xbuf, rsbuf, sbuf, fbuf, ybuf, obuf,
    small_sem, v_sem, a_sem, a_send, a_recv, rs_send, rs_recv, aa_send, aa_recv, out_sem,
):
    pair = lax.axis_index("pair")
    red = lax.axis_index("red")
    core = lax.rem(pair, 2)
    chip = lax.div(pair, 2)
    y = lax.div(chip, NZ)
    z = lax.rem(chip, NZ)
    depth = lhs.shape[1]

    occ_copy = pltpu.make_async_copy(occ_hbm, occs, small_sem.at[0])
    vir_copy = pltpu.make_async_copy(vir_hbm, virv, small_sem.at[1])
    cd_copy = pltpu.make_async_copy(cd_hbm, cdv, small_sem.at[2])
    a_copy = pltpu.make_async_copy(a_hbm, abuf.at[:, core], a_sem)
    occ_copy.start()
    vir_copy.start()
    cd_copy.start()
    a_copy.start()

    barrier = pltpu.get_barrier_semaphore()

    def greet(offset, carry):
        other = lax.rem(chip + offset, NC)
        pl.semaphore_signal(barrier, inc=1, device_id=(other * 2 + core, red), device_id_type=MESH)
        return carry

    pl.semaphore_signal(barrier, inc=1, device_id=(chip * 2 + 1 - core, red), device_id_type=MESH)
    for k in range(1, RED):
        pl.semaphore_signal(barrier, inc=1, device_id=(pair, lax.rem(red + k, RED)), device_id_type=MESH)
    lax.fori_loop(1, NC, greet, 0)

    def load(g, carry):
        for t in range(QG):
            q = chip_at(g * QG + t, y, z)
            start = pl.multiple_of((q * 2 + core) * 128, 128)
            pltpu.make_async_copy(
                v_hbm.at[:, pl.ds(start, 128)], vbuf.at[g, :, pl.ds(128 * t, 128)], v_sem.at[g]
            ).start()
        return carry

    lax.fori_loop(0, STEPS, load, 0)

    pl.semaphore_wait(barrier, 1 + (RED - 1) + (NC - 1))
    a_remote = pltpu.make_async_remote_copy(
        src_ref=a_hbm,
        dst_ref=abuf.at[:, core],
        send_sem=a_send,
        recv_sem=a_recv,
        device_id=(chip * 2 + 1 - core, red),
        device_id_type=MESH,
    )
    a_remote.start()

    vir_copy.wait()
    cd_copy.wait()
    table = virv[...].astype(jnp.float32).astype(jnp.bfloat16)
    width = 512

    def label(i, carry):
        at = pl.ds(pl.multiple_of(i * width, width), width)
        orbitals = cdv[:, at]
        place = lax.broadcasted_iota(jnp.int32, (128, width), 0)
        both = []
        for n in range(2):
            index = orbitals[n : n + 1]
            hot = jnp.where(place == (index & 127), 1.0, 0.0).astype(jnp.bfloat16)
            rows = jnp.dot(table, hot, preferred_element_type=jnp.float32).astype(jnp.int32)
            row = index >> 7
            found = rows[0:1]
            for m in range(1, 4):
                found = jnp.where(row == m, rows[m : m + 1], found)
            both.append(found)
        labels[:, at] = both[0] ^ both[1]
        return carry

    lax.fori_loop(0, depth // width, label, 0)

    occ_copy.wait()
    lane = lax.broadcasted_iota(jnp.int32, (16, 128), 1)
    sub = lax.broadcasted_iota(jnp.int32, (8, 128), 0)
    lane8 = lane[0:8]
    of_lane = (lane >> 5) * 16 + (lane & 15)
    j_irrep = jnp.zeros((16, 128), jnp.int32)
    for j in range(16 * RED):
        j_irrep = jnp.where(of_lane == j, occs[j], j_irrep)
    i_irrep = jnp.where((lane & 16) == 0, occs[2 * chip], occs[2 * chip + 1])
    h_lane = i_irrep ^ j_irrep
    h_rows = jnp.transpose(jnp.broadcast_to(h_lane[0:1].astype(jnp.float32), (128, 128)))
    h_rows = h_rows[:, 0:1].astype(jnp.int32)

    a_copy.wait()
    a_remote.wait()

    def mask(i, carry):
        at = pl.ds(pl.multiple_of(i * width, width), width)
        block = abuf[:, :, :, at].reshape(128, width).astype(jnp.float32)
        keep = h_rows == labels[:, at]
        lhs[:, at] = jnp.where(keep, block, 0.0).astype(jnp.bfloat16)
        return carry

    lax.fori_loop(0, depth // width, mask, 0)

    low64 = lane8 < 64
    low32 = (lane8 & 32) == 0
    low4 = sub < 4

    def red_copy(g, k):
        peer = lax.rem(red + k, RED)
        return pltpu.make_async_remote_copy(
            src_ref=xbuf.at[g, peer],
            dst_ref=rsbuf.at[g, red],
            send_sem=rs_send,
            recv_sem=rs_recv.at[g, red],
            device_id=(pair, peer),
            device_id_type=MESH,
        )

    def multiply(g):
        pltpu.make_async_copy(vbuf.at[g], vbuf.at[g], v_sem.at[g]).wait()
        product = jnp.dot(lhs[...], vbuf[g], preferred_element_type=jnp.float32)
        split = []
        for t in range(QG):
            turned = jnp.transpose(product[:, 128 * t : 128 * (t + 1)])
            kept = turned[0:16]
            for h in range(1, 8):
                kept = jnp.where(h_lane == h, turned[16 * h : 16 * (h + 1)], kept)
            first, second = kept[0:8], kept[8:16]
            split.append((
                jnp.where(low64, first, pltpu.roll(second, 64, 1)),
                jnp.where(low64, pltpu.roll(first, 64, 1), second),
            ))
        for n in range(QG // 2):
            for b in range(2):
                one, two = split[2 * n][b], split[2 * n + 1][b]
                upper = jnp.where(low4, one, pltpu.roll(two, 4, 0))
                lower = jnp.where(low4, pltpu.roll(one, 4, 0), two)
                xbuf[g, 2 * b, n] = jnp.where(low32, upper, pltpu.roll(lower, 32, 1))
                xbuf[g, 2 * b + 1, n] = jnp.where(low32, pltpu.roll(upper, 96, 1), lower)
        for k in range(1, RED):
            red_copy(g, k).start()

    def exchange(g, last):
        for k in range(1, RED):
            source = lax.rem(red + k, RED)
            pltpu.make_async_copy(rsbuf.at[g, source], rsbuf.at[g, source], rs_recv.at[g, source]).wait()
        total = xbuf[g, red]
        for k in range(1, RED):
            total = total + rsbuf[g, lax.rem(red + k, RED)]
        for n in range(QG // 2):
            sbuf[g, 2 * n] = total[n, 0:4]
            sbuf[g, 2 * n + 1] = total[n, 4:8]
        for t in range(QG):
            if last and t == QG - 1:
                fbuf[chip] = total[QG // 2 - 1, 4:8]
            else:
                q = chip_at(g * QG + t, y, z)
                pltpu.make_async_remote_copy(
                    src_ref=sbuf.at[g, t],
                    dst_ref=fbuf.at[chip],
                    send_sem=aa_send,
                    recv_sem=aa_recv,
                    device_id=(q * 2 + core, red),
                    device_id_type=MESH,
                ).start()

    def step(g, carry):
        multiply(g)

        @pl.when(g >= LAG)
        def _():
            exchange(g - LAG, False)

        return carry

    lax.fori_loop(0, STEPS, step, 0)
    for g in range(STEPS - LAG, STEPS):
        exchange(g, g == STEPS - 1)

    jj_irrep = jnp.zeros((16, 128), jnp.int32)
    for j in range(16):
        jj_irrep = jnp.where((lane & 15) == j, occs[16 * red + j], jj_irrep)

    arrived = fbuf.at[pl.ds(0, NC - 1)]
    pltpu.make_async_copy(arrived, arrived, aa_recv).wait()

    def finish(n, carry):
        for m in range(4):
            ybuf[m // 2, 4 * (m % 2) : 4 * (m % 2) + 4] = fbuf[4 * n + m]
        zero, one = ybuf[0], ybuf[1]
        halves = []
        for block in (
            jnp.where(low64, zero, pltpu.roll(one, 64, 1)),
            jnp.where(low64, pltpu.roll(zero, 64, 1), one),
        ):
            swapped = pltpu.roll(block, 4, 0)
            other = jnp.where(low32, pltpu.roll(swapped, 96, 1), pltpu.roll(swapped, 32, 1))
            halves.append(jnp.where(low4 == low32, block, other))
        columns = jnp.concatenate(halves, axis=0)
        of_i = jnp.zeros((16, 128), jnp.int32)
        for i in range(8):
            of_i = jnp.where((lane >> 4) == i, occs[8 * n + i], of_i)
        h_out = of_i ^ jj_irrep
        spread = jnp.concatenate([jnp.where(h_out == h, columns, 0.0) for h in range(8)], axis=0)
        obuf[pl.ds(8 * n, 8)] = jnp.transpose(spread).astype(jnp.bfloat16).reshape(8, 16, 128)
        return carry

    lax.fori_loop(0, NC // 4, finish, 0)
    out_copy = pltpu.make_async_copy(obuf, o_hbm, out_sem)
    out_copy.start()
    sent = xbuf.at[:, pl.ds(0, RED - 1)]
    pltpu.make_async_copy(sent, sent, rs_send).wait()
    pltpu.make_async_copy(arrived, arrived, aa_send).wait()
    out_copy.wait()


def local(amplitudes, integrals, occ_irrep, vir_irrep, cd_orbitals, ab_orbitals):
    depth = integrals.shape[0]
    hbm = pl.BlockSpec(memory_space=pltpu.MemorySpace.HBM)
    return pl.pallas_call(
        kernel,
        out_shape=jax.ShapeDtypeStruct((64, 16, 128), jnp.bfloat16),
        in_specs=[hbm] * 5,
        out_specs=hbm,
        scratch_shapes=[
            pltpu.VMEM((STEPS, depth, QG * 128), jnp.bfloat16),
            pltpu.VMEM((RED, 2, 16, depth), jnp.bfloat16),
            pltpu.VMEM((128, depth), jnp.bfloat16),
            pltpu.VMEM((2, depth), jnp.int32),
            pltpu.VMEM((4, 128), jnp.int32),
            pltpu.SMEM((64,), jnp.int32),
            pltpu.VMEM((1, depth), jnp.int32),
            pltpu.VMEM((STEPS, RED, QG // 2, 8, 128), jnp.float32),
            pltpu.VMEM((STEPS, RED, QG // 2, 8, 128), jnp.float32),
            pltpu.VMEM((STEPS, QG, 4, 128), jnp.float32),
            pltpu.VMEM((NC, 4, 128), jnp.float32),
            pltpu.VMEM((2, 8, 128), jnp.float32),
            pltpu.VMEM((64, 16, 128), jnp.bfloat16),
            pltpu.SemaphoreType.DMA((3,)),
            pltpu.SemaphoreType.DMA((STEPS,)),
            pltpu.SemaphoreType.DMA,
            pltpu.SemaphoreType.DMA,
            pltpu.SemaphoreType.DMA,
            pltpu.SemaphoreType.DMA,
            pltpu.SemaphoreType.DMA((STEPS, RED)),
            pltpu.SemaphoreType.DMA,
            pltpu.SemaphoreType.DMA,
            pltpu.SemaphoreType.DMA,
        ],
        compiler_params=pltpu.CompilerParams(
            collective_id=0, has_side_effects=True, vmem_limit_bytes=48 * 1024 * 1024
        ),
        name="ladder",
    )(
        amplitudes.reshape(RED, 16, depth),
        integrals,
        occ_irrep,
        vir_irrep.reshape(4, 128),
        cd_orbitals,
    )


def solution(mesh):
    in_specs = (P("pair", None, "red"), P("red", None), P(), P(), P(None, "red"), P(None, "pair"))
    out_specs = P(None, "red", "pair")
    return jax.shard_map(local, mesh=mesh, in_specs=in_specs, out_specs=out_specs, check_vma=False)
```

time: 195 us -> 34.4 us (0.18)
  the two profiles are of different devices: /device:TPU:1 before, /device:TPU:8 now
where the time goes in v1:
time: 34.4 us; the launch traced here: 34.2 us
  Pallas kernels  30.5 us (89%)
  local copies, waits for them, and re-layouts  3.71 us (11%)
    pallas_call x1, Pallas kernels, local(): pl.pallas_call(kernel, out_shape=jax.ShapeDtypeStruct((64, 16, 128), jnp....  30.5 us
    unnamed x9, local copies, waits for them, and re-layouts  3.71 us

profile of v1, /device:TPU:8, one launch (start us, length us, event | category | flops | bytes accessed | tf_op | source)
XLA Modules:
  0.0 34.2 jit_solution(11270710102828691164)
XLA Ops:
  0.0 0.0 copy-start
  0.0 0.9 %copy-done = bf16[1,64,2048]{2,1,0:T(8,128)(2,1)S(1)} copy-done((bf16[1,64,2048]{2,1,0:T(8,128)(2,1)S(1)}, bf16[1,64,2048]{2,1,0:T(8,128)(2,1)}, u32[]{:S(2)}) %copy-start) | copy-done | bytes 262168
  1.0 0.0 copy-start.1
  1.0 0.7 %copy-done.1 = s32[2,2048]{1,0:T(2,128)S(1)} copy-done((s32[2,2048]{1,0:T(2,128)S(1)}, s32[2,2048]{1,0:T(2,128)}, u32[]{:S(2)}) %copy-start.1) | copy-done | bytes 16408
  1.7 0.0 copy-start.2
  1.7 0.7 %copy-done.2 = s32[512]{0:T(512)S(1)} copy-done((s32[512]{0:T(512)S(1)}, s32[512]{0:T(512)}, u32[]{:S(2)}) %copy-start.2) | copy-done | bytes 2072
  2.4 0.0 copy-start.3
  2.4 0.7 %copy-done.3 = s32[64]{0:T(128)S(1)} copy-done((s32[64]{0:T(128)S(1)}, s32[64]{0:T(128)}, u32[]{:S(2)}) %copy-start.3) | copy-done | bytes 280
  3.0 30.5 %ladder.1 = bf16[64,16,128]{2,1,0:T(8,128)(2,1)S(1)} custom-call(bf16[4,16,2048]{2,1,0:T(8,128)(2,1)S(1)} %bitcast.2, bf16[2048,8192]{1,0:T(8,128)(2,1)} %v_hbm.1, s32[64]{0:T(128)S(1)} %copy-done.3, s32[4,128]{1,0:T(4,128)S(1)} %bitcast.3, s32[2,2048]{1,0:T(2,128)S(1)} %copy-done.1), custom_call_target="tpu_custom_call" | custom-call | tf_op jit(solution)/shard_map/ladder/pallas_call | solution.py:252
  33.5 0.7 %copy.7 = bf16[64,16,128]{2,1,0:T(8,128)(2,1)} copy(bf16[64,16,128]{2,1,0:T(8,128)(2,1)S(1)} %ladder.1) | data formatting | bytes 524288
Async XLA Ops:
  0.0 0.9 %copy-start = (bf16[1,64,2048]{2,1,0:T(8,128)(2,1)S(1)}, bf16[1,64,2048]{2,1,0:T(8,128)(2,1)}, u32[]{:S(2)}) copy-start(bf16[1,64,2048]{2,1,0:T(8,128)(2,1)} %param.6) | copy-start | bytes 786436
  1.0 0.7 %copy-start.1 = (s32[2,2048]{1,0:T(2,128)S(1)}, s32[2,2048]{1,0:T(2,128)}, u32[]{:S(2)}) copy-start(s32[2,2048]{1,0:T(2,128)} %cd_hbm.1) | copy-start | bytes 49156
  1.7 0.7 %copy-start.2 = (s32[512]{0:T(512)S(1)}, s32[512]{0:T(512)}, u32[]{:S(2)}) copy-start(s32[512]{0:T(512)} %param.9) | copy-start | bytes 6148
  2.4 0.7 %copy-start.3 = (s32[64]{0:T(128)S(1)}, s32[64]{0:T(128)}, u32[]{:S(2)}) copy-start(s32[64]{0:T(128)} %occ_hbm.1) | copy-start | bytes 772

commit v2 on v1

--- a/solution.py
+++ b/solution.py
@@ -12,7 +12,6 @@
 RED = 4
 QG = 4
 STEPS = NC // QG
-LAG = 2
 MESH = pl.DeviceIdType.MESH
 
 
@@ -31,7 +30,7 @@
 def kernel(
     a_hbm, v_hbm, occ_hbm, vir_hbm, cd_hbm, o_hbm,
     vbuf, abuf, lhs, cdv, virv, occs, labels, xbuf, rsbuf, sbuf, fbuf, ybuf, obuf,
-    small_sem, v_sem, a_sem, a_send, a_recv, rs_send, rs_recv, aa_send, aa_recv, out_sem,
+    late_sem, small_sem, v_sem, a_sem, a_send, a_recv, rs_send, rs_recv, aa_send, aa_recv, out_sem,
 ):
     pair = lax.axis_index("pair")
     red = lax.axis_index("red")
@@ -51,16 +50,13 @@
     a_copy.start()
 
     barrier = pltpu.get_barrier_semaphore()
-
-    def greet(offset, carry):
-        other = lax.rem(chip + offset, NC)
-        pl.semaphore_signal(barrier, inc=1, device_id=(other * 2 + core, red), device_id_type=MESH)
-        return carry
-
-    pl.semaphore_signal(barrier, inc=1, device_id=(chip * 2 + 1 - core, red), device_id_type=MESH)
-    for k in range(1, RED):
-        pl.semaphore_signal(barrier, inc=1, device_id=(pair, lax.rem(red + k, RED)), device_id_type=MESH)
-    lax.fori_loop(1, NC, greet, 0)
+    partner = (chip * 2 + 1 - core, red)
+    y_peers = [((lax.rem(y + k, NY) * NZ + z) * 2 + core, red) for k in range(1, NY)]
+    z_peers = [((y * NZ + lax.rem(z + k, NZ)) * 2 + core, red) for k in range(1, NZ)]
+    red_peers = [(pair, lax.rem(red + k, RED)) for k in range(1, RED)]
+    greeted = [partner] + red_peers + y_peers + z_peers
+    for peer in greeted:
+        pl.semaphore_signal(barrier, inc=1, device_id=peer, device_id_type=MESH)
 
     def load(g, carry):
         for t in range(QG):
@@ -73,16 +69,18 @@
 
     lax.fori_loop(0, STEPS, load, 0)
 
-    pl.semaphore_wait(barrier, 1 + (RED - 1) + (NC - 1))
+    pl.semaphore_wait(barrier, len(greeted))
     a_remote = pltpu.make_async_remote_copy(
         src_ref=a_hbm,
         dst_ref=abuf.at[:, core],
         send_sem=a_send,
         recv_sem=a_recv,
-        device_id=(chip * 2 + 1 - core, red),
+        device_id=partner,
         device_id_type=MESH,
     )
     a_remote.start()
+    for peer in y_peers:
+        pl.semaphore_signal(late_sem, inc=1, device_id=peer, device_id_type=MESH)
 
     vir_copy.wait()
     cd_copy.wait()
@@ -198,16 +196,18 @@
 
     def step(g, carry):
         multiply(g)
-
-        @pl.when(g >= LAG)
-        def _():
-            exchange(g - LAG, False)
-
         return carry
 
     lax.fori_loop(0, STEPS, step, 0)
-    for g in range(STEPS - LAG, STEPS):
-        exchange(g, g == STEPS - 1)
+
+    pl.semaphore_wait(late_sem, NY - 1)
+
+    def pass_on(g, carry):
+        exchange(g, False)
+        return carry
+
+    lax.fori_loop(0, STEPS - 1, pass_on, 0)
+    exchange(STEPS - 1, True)
 
     jj_irrep = jnp.zeros((16, 128), jnp.int32)
     for j in range(16):
@@ -268,6 +268,7 @@
             pltpu.VMEM((NC, 4, 128), jnp.float32),
             pltpu.VMEM((2, 8, 128), jnp.float32),
             pltpu.VMEM((64, 16, 128), jnp.bfloat16),
+            pltpu.SemaphoreType.REGULAR,
             pltpu.SemaphoreType.DMA((3,)),
             pltpu.SemaphoreType.DMA((STEPS,)),
             pltpu.SemaphoreType.DMA,
@@ -280,7 +281,7 @@
             pltpu.SemaphoreType.DMA,
         ],
         compiler_params=pltpu.CompilerParams(
-            collective_id=0, has_side_effects=True, vmem_limit_bytes=48 * 1024 * 1024
+            collective_id=0, has_side_effects=True, vmem_limit_bytes=56 * 1024 * 1024
         ),
         name="ladder",
     )(

time: 34.4 us -> 28.2 us (0.82)
  the two profiles are of different devices: /device:TPU:8 before, /device:TPU:1 now
where the time goes in v2:
time: 28.2 us; the launch traced here: 28.1 us
  Pallas kernels  26.4 us (94%)
  local copies, waits for them, and re-layouts  1.67 us (6%)
    pallas_call x1, Pallas kernels, local(): pl.pallas_call(kernel, out_shape=jax.ShapeDtypeStruct((64, 16, 128), jnp....  26.4 us
    unnamed x1, local copies, waits for them, and re-layouts  1.67 us

profile of v2, /device:TPU:1, one launch (start us, length us, event | category | flops | bytes accessed | tf_op | source)
XLA Modules:
  0.0 28.1 jit_solution(14829480584305185579)
XLA Ops:
  0.0 26.4 %ladder.1 = bf16[64,16,128]{2,1,0:T(8,128)(2,1)} custom-call(bf16[4,16,2048]{2,1,0:T(8,128)(2,1)} %bitcast.2, bf16[2048,8192]{1,0:T(8,128)(2,1)} %v_hbm.1, s32[64]{0:T(128)} %occ_hbm.1, s32[4,128]{1,0:T(4,128)} %bitcast.3, s32[2,2048]{1,0:T(2,128)} %cd_hbm.1), custom_call_target="tpu_custom_call" | custom-call | tf_op jit(solution)/shard_map/ladder/pallas_call | solution.py:252
  26.4 1.7 %copy.7 = bf16[64,16,128]{2,1,0:T(8,128)(2,1)} copy(bf16[64,16,128]{2,1,0:T(8,128)(2,1)} %ladder.1) | data formatting | bytes 524288

commit v3 on v2

--- a/solution.py
+++ b/solution.py
@@ -10,7 +10,8 @@
 NY, NZ = 4, 8
 NC = NY * NZ
 RED = 4
-QG = 4
+QG = NY
+LAG = 4
 STEPS = NC // QG
 MESH = pl.DeviceIdType.MESH
 
@@ -22,9 +23,13 @@
 
 def chip_at(step, y, z):
     offset = NC - 1 - step
-    dz = zigzag(lax.rem(offset, NZ))
-    dy = zigzag(lax.div(offset, NZ))
+    dz = zigzag(lax.div(offset, NY))
+    dy = zigzag(lax.rem(offset, NY))
     return lax.rem(y + dy + NY, NY) * NZ + lax.rem(z + dz + NZ, NZ)
+
+
+def ring_distance(place, size):
+    return jnp.minimum(place, size - place)
 
 
 def kernel(
@@ -71,13 +76,14 @@
 
     pl.semaphore_wait(barrier, len(greeted))
     a_remote = pltpu.make_async_remote_copy(
-        src_ref=a_hbm,
+        src_ref=abuf.at[:, core],
         dst_ref=abuf.at[:, core],
         send_sem=a_send,
         recv_sem=a_recv,
         device_id=partner,
         device_id_type=MESH,
     )
+    a_copy.wait()
     a_remote.start()
     for peer in y_peers:
         pl.semaphore_signal(late_sem, inc=1, device_id=peer, device_id_type=MESH)
@@ -119,7 +125,6 @@
     h_rows = jnp.transpose(jnp.broadcast_to(h_lane[0:1].astype(jnp.float32), (128, 128)))
     h_rows = h_rows[:, 0:1].astype(jnp.int32)
 
-    a_copy.wait()
     a_remote.wait()
 
     def mask(i, carry):
@@ -182,43 +187,55 @@
             sbuf[g, 2 * n + 1] = total[n, 4:8]
         for t in range(QG):
             if last and t == QG - 1:
-                fbuf[chip] = total[QG // 2 - 1, 4:8]
+                pltpu.make_async_copy(sbuf.at[g, t], fbuf.at[z, y], aa_recv.at[z]).start()
             else:
                 q = chip_at(g * QG + t, y, z)
                 pltpu.make_async_remote_copy(
                     src_ref=sbuf.at[g, t],
-                    dst_ref=fbuf.at[chip],
+                    dst_ref=fbuf.at[z, y],
                     send_sem=aa_send,
-                    recv_sem=aa_recv,
+                    recv_sem=aa_recv.at[z],
                     device_id=(q * 2 + core, red),
                     device_id_type=MESH,
                 ).start()
 
+    far = ring_distance(red, RED) + ring_distance(y, NY) + ring_distance(z, NZ) >= 5
+
     def step(g, carry):
+        @pl.when(far & (g == LAG))
+        def _():
+            pl.semaphore_wait(late_sem, NY - 1)
+
+        @pl.when(far & (g >= LAG))
+        def _():
+            exchange(g - LAG, False)
+
         multiply(g)
         return carry
 
     lax.fori_loop(0, STEPS, step, 0)
 
-    pl.semaphore_wait(late_sem, NY - 1)
+    @pl.when(jnp.logical_not(far))
+    def _():
+        pl.semaphore_wait(late_sem, NY - 1)
 
     def pass_on(g, carry):
         exchange(g, False)
         return carry
 
-    lax.fori_loop(0, STEPS - 1, pass_on, 0)
+    lax.fori_loop(jnp.where(far, STEPS - LAG, 0), STEPS - 1, pass_on, 0)
     exchange(STEPS - 1, True)
 
     jj_irrep = jnp.zeros((16, 128), jnp.int32)
     for j in range(16):
         jj_irrep = jnp.where((lane & 15) == j, occs[16 * red + j], jj_irrep)
 
-    arrived = fbuf.at[pl.ds(0, NC - 1)]
-    pltpu.make_async_copy(arrived, arrived, aa_recv).wait()
-
     def finish(n, carry):
-        for m in range(4):
-            ybuf[m // 2, 4 * (m % 2) : 4 * (m % 2) + 4] = fbuf[4 * n + m]
+        of_z = lax.rem(z + zigzag(n) + NZ, NZ)
+        arrived = fbuf.at[of_z]
+        pltpu.make_async_copy(arrived, arrived, aa_recv.at[of_z]).wait()
+        for m in range(NY):
+            ybuf[m // 2, 4 * (m % 2) : 4 * (m % 2) + 4] = fbuf[of_z, m]
         zero, one = ybuf[0], ybuf[1]
         halves = []
         for block in (
@@ -231,19 +248,19 @@
         columns = jnp.concatenate(halves, axis=0)
         of_i = jnp.zeros((16, 128), jnp.int32)
         for i in range(8):
-            of_i = jnp.where((lane >> 4) == i, occs[8 * n + i], of_i)
+            of_i = jnp.where((lane >> 4) == i, occs[2 * NZ * (i // 2) + 2 * of_z + i % 2], of_i)
         h_out = of_i ^ jj_irrep
         spread = jnp.concatenate([jnp.where(h_out == h, columns, 0.0) for h in range(8)], axis=0)
-        obuf[pl.ds(8 * n, 8)] = jnp.transpose(spread).astype(jnp.bfloat16).reshape(8, 16, 128)
-        return carry
-
-    lax.fori_loop(0, NC // 4, finish, 0)
-    out_copy = pltpu.make_async_copy(obuf, o_hbm, out_sem)
-    out_copy.start()
+        obuf[:, of_z] = jnp.transpose(spread).astype(jnp.bfloat16).reshape(NY, 32, 128)
+        pltpu.make_async_copy(obuf.at[:, of_z], o_hbm.at[:, of_z], out_sem).start()
+        return carry
+
+    lax.fori_loop(0, NZ, finish, 0)
     sent = xbuf.at[:, pl.ds(0, RED - 1)]
     pltpu.make_async_copy(sent, sent, rs_send).wait()
-    pltpu.make_async_copy(arrived, arrived, aa_send).wait()
-    out_copy.wait()
+    all_sent = sbuf.reshape(NC, 4, 128).at[pl.ds(0, NC - 1)]
+    pltpu.make_async_copy(all_sent, all_sent, aa_send).wait()
+    pltpu.make_async_copy(obuf, o_hbm, out_sem).wait()
 
 
 def local(amplitudes, integrals, occ_irrep, vir_irrep, cd_orbitals, ab_orbitals):
@@ -251,7 +268,7 @@
     hbm = pl.BlockSpec(memory_space=pltpu.MemorySpace.HBM)
     return pl.pallas_call(
         kernel,
-        out_shape=jax.ShapeDtypeStruct((64, 16, 128), jnp.bfloat16),
+        out_shape=jax.ShapeDtypeStruct((NY, NZ, 32, 128), jnp.bfloat16),
         in_specs=[hbm] * 5,
         out_specs=hbm,
         scratch_shapes=[
@@ -265,9 +282,9 @@
             pltpu.VMEM((STEPS, RED, QG // 2, 8, 128), jnp.float32),
             pltpu.VMEM((STEPS, RED, QG // 2, 8, 128), jnp.float32),
             pltpu.VMEM((STEPS, QG, 4, 128), jnp.float32),
-            pltpu.VMEM((NC, 4, 128), jnp.float32),
+            pltpu.VMEM((NZ, NY, 4, 128), jnp.float32),
             pltpu.VMEM((2, 8, 128), jnp.float32),
-            pltpu.VMEM((64, 16, 128), jnp.bfloat16),
+            pltpu.VMEM((NY, NZ, 32, 128), jnp.bfloat16),
             pltpu.SemaphoreType.REGULAR,
             pltpu.SemaphoreType.DMA((3,)),
             pltpu.SemaphoreType.DMA((STEPS,)),
@@ -277,7 +294,7 @@
             pltpu.SemaphoreType.DMA,
             pltpu.SemaphoreType.DMA((STEPS, RED)),
             pltpu.SemaphoreType.DMA,
-            pltpu.SemaphoreType.DMA,
+            pltpu.SemaphoreType.DMA((NZ,)),
             pltpu.SemaphoreType.DMA,
         ],
         compiler_params=pltpu.CompilerParams(
@@ -290,7 +307,7 @@
         occ_irrep,
         vir_irrep.reshape(4, 128),
         cd_orbitals,
-    )
+    ).reshape(64, 16, 128)
 
 
 def solution(mesh):

time: 28.2 us -> 29 us (1.028)
  Pallas kernels: 26.4 us -> 27.2 us
    pallas_call x1, Pallas kernels: 26.4 us -> 27.2 us  [local(): pl.pallas_call(kernel, out_shape=jax.ShapeDtypeStruct((NY, NZ, 32, 128),...]
where the time goes in v3:
time: 29 us; the launch traced here: 28.9 us
  Pallas kernels  27.2 us (94%)
  local copies, waits for them, and re-layouts  1.67 us (6%)
    pallas_call x1, Pallas kernels, local(): pl.pallas_call(kernel, out_shape=jax.ShapeDtypeStruct((NY, NZ, 32, 128),...  27.2 us
    unnamed x1, local copies, waits for them, and re-layouts  1.67 us

profile of v3, /device:TPU:1, one launch (start us, length us, event | category | flops | bytes accessed | tf_op | source)
XLA Modules:
  0.0 28.9 jit_solution(11045132918612944665)
XLA Ops:
  0.0 27.2 %ladder.1 = bf16[4,8,32,128]{3,2,1,0:T(8,128)(2,1)} custom-call(bf16[4,16,2048]{2,1,0:T(8,128)(2,1)} %bitcast.4, bf16[2048,8192]{1,0:T(8,128)(2,1)} %v_hbm.1, s32[64]{0:T(128)} %occ_hbm.1, s32[4,128]{1,0:T(4,128)} %bitcast.5, s32[2,2048]{1,0:T(2,128)} %cd_hbm.1), custom_call_target="tpu_custom_call" | custom-call | tf_op jit(solution)/shard_map/ladder/pallas_call | solution.py:269
  27.2 1.7 %copy.7 = bf16[64,16,128]{2,1,0:T(8,128)(2,1)} copy(bf16[64,16,128]{2,1,0:T(8,128)(2,1)} %bitcast.3) | data formatting | bytes 524288

commit v4 on v3

--- a/solution.py
+++ b/solution.py
@@ -11,7 +11,7 @@
 NC = NY * NZ
 RED = 4
 QG = NY
-LAG = 4
+LAG = 5
 STEPS = NC // QG
 MESH = pl.DeviceIdType.MESH
 
@@ -35,7 +35,7 @@
 def kernel(
     a_hbm, v_hbm, occ_hbm, vir_hbm, cd_hbm, o_hbm,
     vbuf, abuf, lhs, cdv, virv, occs, labels, xbuf, rsbuf, sbuf, fbuf, ybuf, obuf,
-    late_sem, small_sem, v_sem, a_sem, a_send, a_recv, rs_send, rs_recv, aa_send, aa_recv, out_sem,
+    z_sem, late_sem, small_sem, v_sem, a_sem, a_send, a_recv, rs_send, rs_recv, aa_send, aa_recv, out_sem,
 ):
     pair = lax.axis_index("pair")
     red = lax.axis_index("red")
@@ -57,7 +57,7 @@
     barrier = pltpu.get_barrier_semaphore()
     partner = (chip * 2 + 1 - core, red)
     y_peers = [((lax.rem(y + k, NY) * NZ + z) * 2 + core, red) for k in range(1, NY)]
-    z_peers = [((y * NZ + lax.rem(z + k, NZ)) * 2 + core, red) for k in range(1, NZ)]
+    z_peers = [((y * NZ + lax.rem(z + k, NZ)) * 2 + core, red) for k in (1, NZ - 1, 2, NZ - 2)]
     red_peers = [(pair, lax.rem(red + k, RED)) for k in range(1, RED)]
     greeted = [partner] + red_peers + y_peers + z_peers
     for peer in greeted:
@@ -85,8 +85,8 @@
     )
     a_copy.wait()
     a_remote.start()
-    for peer in y_peers:
-        pl.semaphore_signal(late_sem, inc=1, device_id=peer, device_id_type=MESH)
+    for peer in z_peers[2:]:
+        pl.semaphore_signal(z_sem, inc=1, device_id=peer, device_id_type=MESH)
 
     vir_copy.wait()
     cd_copy.wait()
@@ -202,6 +202,12 @@
     far = ring_distance(red, RED) + ring_distance(y, NY) + ring_distance(z, NZ) >= 5
 
     def step(g, carry):
+        @pl.when(g == 2)
+        def _():
+            pl.semaphore_wait(z_sem, 2)
+            for peer in y_peers:
+                pl.semaphore_signal(late_sem, inc=1, device_id=peer, device_id_type=MESH)
+
         @pl.when(far & (g == LAG))
         def _():
             pl.semaphore_wait(late_sem, NY - 1)
@@ -219,24 +225,26 @@
     def _():
         pl.semaphore_wait(late_sem, NY - 1)
 
-    def pass_on(g, carry):
-        exchange(g, False)
-        return carry
-
-    lax.fori_loop(jnp.where(far, STEPS - LAG, 0), STEPS - 1, pass_on, 0)
+    def pass_on(n, carry):
+        exchange(STEPS - 2 - n, False)
+        return carry
+
     exchange(STEPS - 1, True)
+    lax.fori_loop(0, jnp.where(far, LAG - 1, STEPS - 1), pass_on, 0)
 
     jj_irrep = jnp.zeros((16, 128), jnp.int32)
     for j in range(16):
         jj_irrep = jnp.where((lane & 15) == j, occs[16 * red + j], jj_irrep)
 
-    def finish(n, carry):
-        of_z = lax.rem(z + zigzag(n) + NZ, NZ)
-        arrived = fbuf.at[of_z]
-        pltpu.make_async_copy(arrived, arrived, aa_recv.at[of_z]).wait()
+    def arrive(n, carry):
+        arrived = fbuf.at[n]
+        pltpu.make_async_copy(arrived, arrived, aa_recv.at[n]).wait()
+        return carry
+
+    def finish(n):
         for m in range(NY):
-            ybuf[m // 2, 4 * (m % 2) : 4 * (m % 2) + 4] = fbuf[of_z, m]
-        zero, one = ybuf[0], ybuf[1]
+            ybuf[n, m // 2, 4 * (m % 2) : 4 * (m % 2) + 4] = fbuf[n, m]
+        zero, one = ybuf[n, 0], ybuf[n, 1]
         halves = []
         for block in (
             jnp.where(low64, zero, pltpu.roll(one, 64, 1)),
@@ -248,19 +256,21 @@
         columns = jnp.concatenate(halves, axis=0)
         of_i = jnp.zeros((16, 128), jnp.int32)
         for i in range(8):
-            of_i = jnp.where((lane >> 4) == i, occs[2 * NZ * (i // 2) + 2 * of_z + i % 2], of_i)
+            of_i = jnp.where((lane >> 4) == i, occs[2 * NZ * (i // 2) + 2 * n + i % 2], of_i)
         h_out = of_i ^ jj_irrep
         spread = jnp.concatenate([jnp.where(h_out == h, columns, 0.0) for h in range(8)], axis=0)
-        obuf[:, of_z] = jnp.transpose(spread).astype(jnp.bfloat16).reshape(NY, 32, 128)
-        pltpu.make_async_copy(obuf.at[:, of_z], o_hbm.at[:, of_z], out_sem).start()
-        return carry
-
-    lax.fori_loop(0, NZ, finish, 0)
+        obuf[:, n] = jnp.transpose(spread).astype(jnp.bfloat16).reshape(NY, 32, 128)
+
+    lax.fori_loop(0, NZ, arrive, 0)
+    for n in range(NZ):
+        finish(n)
+    out_copy = pltpu.make_async_copy(obuf, o_hbm, out_sem)
+    out_copy.start()
     sent = xbuf.at[:, pl.ds(0, RED - 1)]
     pltpu.make_async_copy(sent, sent, rs_send).wait()
     all_sent = sbuf.reshape(NC, 4, 128).at[pl.ds(0, NC - 1)]
     pltpu.make_async_copy(all_sent, all_sent, aa_send).wait()
-    pltpu.make_async_copy(obuf, o_hbm, out_sem).wait()
+    out_copy.wait()
 
 
 def local(amplitudes, integrals, occ_irrep, vir_irrep, cd_orbitals, ab_orbitals):
@@ -283,8 +293,9 @@
             pltpu.VMEM((STEPS, RED, QG // 2, 8, 128), jnp.float32),
             pltpu.VMEM((STEPS, QG, 4, 128), jnp.float32),
             pltpu.VMEM((NZ, NY, 4, 128), jnp.float32),
-            pltpu.VMEM((2, 8, 128), jnp.float32),
+            pltpu.VMEM((NZ, 2, 8, 128), jnp.float32),
             pltpu.VMEM((NY, NZ, 32, 128), jnp.bfloat16),
+            pltpu.SemaphoreType.REGULAR,
             pltpu.SemaphoreType.REGULAR,
             pltpu.SemaphoreType.DMA((3,)),
             pltpu.SemaphoreType.DMA((STEPS,)),
@@ -298,15 +309,20 @@
             pltpu.SemaphoreType.DMA,
         ],
         compiler_params=pltpu.CompilerParams(
-            collective_id=0, has_side_effects=True, vmem_limit_bytes=56 * 1024 * 1024
+            collective_id=0, has_side_effects=True, vmem_limit_bytes=40 * 1024 * 1024
         ),
         name="ladder",
     )(
-        amplitudes.reshape(RED, 16, depth),
-        integrals,
-        occ_irrep,
-        vir_irrep.reshape(4, 128),
-        cd_orbitals,
+        *(
+            pltpu.with_memory_space_constraint(operand, pltpu.MemorySpace.HBM)
+            for operand in (
+                amplitudes.reshape(RED, 16, depth),
+                integrals,
+                occ_irrep,
+                vir_irrep.reshape(4, 128),
+                cd_orbitals,
+            )
+        )
     ).reshape(64, 16, 128)
 
 

time: 29 us -> 27.3 us (0.941)
  the two profiles are of different devices: /device:TPU:1 before, /device:TPU:32 now
where the time goes in v4:
time: 27.3 us; the launch traced here: 27.2 us
  Pallas kernels  26.5 us (97%)
  local copies, waits for them, and re-layouts  0.71 us (3%)
    pallas_call x1, Pallas kernels, local(): pl.pallas_call(kernel, out_shape=jax.ShapeDtypeStruct((NY, NZ, 32, 128),...  26.5 us
    unnamed x1, local copies, waits for them, and re-layouts  0.71 us

profile of v4, /device:TPU:32, one launch (start us, length us, event | category | flops | bytes accessed | tf_op | source)
XLA Modules:
  0.0 27.2 jit_solution(11939502939895739034)
XLA Ops:
  0.0 26.5 %ladder.1 = bf16[4,8,32,128]{3,2,1,0:T(8,128)(2,1)S(1)} custom-call(bf16[4,16,2048]{2,1,0:T(8,128)(2,1)} %bitcast.4, bf16[2048,8192]{1,0:T(8,128)(2,1)} %v_hbm.1, s32[64]{0:T(128)} %occ_hbm.1, s32[4,128]{1,0:T(4,128)} %bitcast.5, s32[2,2048]{1,0:T(2,128)} %cd_hbm.1), custom_call_target="tpu_custom_call" | custom-call | tf_op jit(solution)/shard_map/ladder/pallas_call | solution.py:279
  26.5 0.7 %copy.7 = bf16[64,16,128]{2,1,0:T(8,128)(2,1)} copy(bf16[64,16,128]{2,1,0:T(8,128)(2,1)S(1)} %bitcast.3) | data formatting | bytes 524288

commit v5 on v4

--- a/solution.py
+++ b/solution.py
@@ -11,25 +11,8 @@
 NC = NY * NZ
 RED = 4
 QG = NY
-LAG = 5
 STEPS = NC // QG
 MESH = pl.DeviceIdType.MESH
-
-
-def zigzag(t):
-    half = lax.div(t + 1, 2)
-    return half * (1 - 2 * lax.rem(t + 1, 2))
-
-
-def chip_at(step, y, z):
-    offset = NC - 1 - step
-    dz = zigzag(lax.div(offset, NY))
-    dy = zigzag(lax.rem(offset, NY))
-    return lax.rem(y + dy + NY, NY) * NZ + lax.rem(z + dz + NZ, NZ)
-
-
-def ring_distance(place, size):
-    return jnp.minimum(place, size - place)
 
 
 def kernel(
@@ -65,8 +48,7 @@
 
     def load(g, carry):
         for t in range(QG):
-            q = chip_at(g * QG + t, y, z)
-            start = pl.multiple_of((q * 2 + core) * 128, 128)
+            start = pl.multiple_of(((t * NZ + g) * 2 + core) * 128, 128)
             pltpu.make_async_copy(
                 v_hbm.at[:, pl.ds(start, 128)], vbuf.at[g, :, pl.ds(128 * t, 128)], v_sem.at[g]
             ).start()
@@ -175,7 +157,7 @@
         for k in range(1, RED):
             red_copy(g, k).start()
 
-    def exchange(g, last):
+    def exchange(g, carry):
         for k in range(1, RED):
             source = lax.rem(red + k, RED)
             pltpu.make_async_copy(rsbuf.at[g, source], rsbuf.at[g, source], rs_recv.at[g, source]).wait()
@@ -186,51 +168,39 @@
             sbuf[g, 2 * n] = total[n, 0:4]
             sbuf[g, 2 * n + 1] = total[n, 4:8]
         for t in range(QG):
-            if last and t == QG - 1:
-                pltpu.make_async_copy(sbuf.at[g, t], fbuf.at[z, y], aa_recv.at[z]).start()
-            else:
-                q = chip_at(g * QG + t, y, z)
+            own = (y == t) & (z == g)
+
+            @pl.when(own)
+            def _():
+                pltpu.make_async_copy(sbuf.at[g, t], fbuf.at[g, t], aa_recv.at[g]).start()
+
+            @pl.when(jnp.logical_not(own))
+            def _():
                 pltpu.make_async_remote_copy(
                     src_ref=sbuf.at[g, t],
                     dst_ref=fbuf.at[z, y],
                     send_sem=aa_send,
                     recv_sem=aa_recv.at[z],
-                    device_id=(q * 2 + core, red),
+                    device_id=((t * NZ + g) * 2 + core, red),
                     device_id_type=MESH,
                 ).start()
 
-    far = ring_distance(red, RED) + ring_distance(y, NY) + ring_distance(z, NZ) >= 5
+        return carry
 
     def step(g, carry):
-        @pl.when(g == 2)
+        @pl.when(g == 3)
         def _():
             pl.semaphore_wait(z_sem, 2)
             for peer in y_peers:
                 pl.semaphore_signal(late_sem, inc=1, device_id=peer, device_id_type=MESH)
 
-        @pl.when(far & (g == LAG))
-        def _():
-            pl.semaphore_wait(late_sem, NY - 1)
-
-        @pl.when(far & (g >= LAG))
-        def _():
-            exchange(g - LAG, False)
-
         multiply(g)
         return carry
 
     lax.fori_loop(0, STEPS, step, 0)
 
-    @pl.when(jnp.logical_not(far))
-    def _():
-        pl.semaphore_wait(late_sem, NY - 1)
-
-    def pass_on(n, carry):
-        exchange(STEPS - 2 - n, False)
-        return carry
-
-    exchange(STEPS - 1, True)
-    lax.fori_loop(0, jnp.where(far, LAG - 1, STEPS - 1), pass_on, 0)
+    pl.semaphore_wait(late_sem, NY - 1)
+    lax.fori_loop(0, STEPS, exchange, 0)
 
     jj_irrep = jnp.zeros((16, 128), jnp.int32)
     for j in range(16):

time: 27.3 us -> 23.9 us (0.88)
  the two profiles are of different devices: /device:TPU:32 before, /device:TPU:1 now
where the time goes in v5:
time: 23.9 us; the launch traced here: 23.8 us
  Pallas kernels  23.1 us (97%)
  local copies, waits for them, and re-layouts  0.71 us (3%)
    pallas_call x1, Pallas kernels, local(): pl.pallas_call(kernel, out_shape=jax.ShapeDtypeStruct((NY, NZ, 32, 128),...  23.1 us
    unnamed x1, local copies, waits for them, and re-layouts  0.71 us

profile of v5, /device:TPU:1, one launch (start us, length us, event | category | flops | bytes accessed | tf_op | source)
XLA Modules:
  0.0 23.8 jit_solution(358318177243235269)
XLA Ops:
  0.0 23.1 %ladder.1 = bf16[4,8,32,128]{3,2,1,0:T(8,128)(2,1)S(1)} custom-call(bf16[4,16,2048]{2,1,0:T(8,128)(2,1)} %bitcast.4, bf16[2048,8192]{1,0:T(8,128)(2,1)} %v_hbm.1, s32[64]{0:T(128)} %occ_hbm.1, s32[4,128]{1,0:T(4,128)} %bitcast.5, s32[2,2048]{1,0:T(2,128)} %cd_hbm.1), custom_call_target="tpu_custom_call" | custom-call | tf_op jit(solution)/shard_map/ladder/pallas_call | solution.py:249
  23.1 0.7 %copy.7 = bf16[64,16,128]{2,1,0:T(8,128)(2,1)} copy(bf16[64,16,128]{2,1,0:T(8,128)(2,1)S(1)} %bitcast.3) | data formatting | bytes 524288

commit v6 on v5

--- a/solution.py
+++ b/solution.py
@@ -12,13 +12,18 @@
 RED = 4
 QG = NY
 STEPS = NC // QG
+LAG = 5
 MESH = pl.DeviceIdType.MESH
+
+
+def start_key(of_y, of_z, chip):
+    return (of_y + of_z) * NC + chip
 
 
 def kernel(
     a_hbm, v_hbm, occ_hbm, vir_hbm, cd_hbm, o_hbm,
     vbuf, abuf, lhs, cdv, virv, occs, labels, xbuf, rsbuf, sbuf, fbuf, ybuf, obuf,
-    z_sem, late_sem, small_sem, v_sem, a_sem, a_send, a_recv, rs_send, rs_recv, aa_send, aa_recv, out_sem,
+    late_sem, small_sem, v_sem, a_sem, a_send, a_recv, rs_send, rs_recv, aa_send, aa_recv, out_sem,
 ):
     pair = lax.axis_index("pair")
     red = lax.axis_index("red")
@@ -39,12 +44,24 @@
 
     barrier = pltpu.get_barrier_semaphore()
     partner = (chip * 2 + 1 - core, red)
-    y_peers = [((lax.rem(y + k, NY) * NZ + z) * 2 + core, red) for k in range(1, NY)]
-    z_peers = [((y * NZ + lax.rem(z + k, NZ)) * 2 + core, red) for k in (1, NZ - 1, 2, NZ - 2)]
     red_peers = [(pair, lax.rem(red + k, RED)) for k in range(1, RED)]
-    greeted = [partner] + red_peers + y_peers + z_peers
-    for peer in greeted:
+    own_key = start_key(jnp.where(y < 2, 11 * y, 3 * y + 15), jnp.where(z < 4, 9 * z, z + 27), chip)
+    keys = [
+        start_key(11 * t if t < 2 else 3 * t + 15, 9 * m if m < 4 else m + 27, t * NZ + m)
+        for t in range(NY)
+        for m in range(NZ)
+    ]
+
+    def count(conditions):
+        return sum(jnp.where(condition, 1, 0) for condition in conditions)
+
+    for peer in [partner] + red_peers:
         pl.semaphore_signal(barrier, inc=1, device_id=peer, device_id_type=MESH)
+    for other in range(NC):
+
+        @pl.when(own_key < keys[other])
+        def _(other=other):
+            pl.semaphore_signal(barrier, inc=1, device_id=(other * 2 + core, red), device_id_type=MESH)
 
     def load(g, carry):
         for t in range(QG):
@@ -56,7 +73,7 @@
 
     lax.fori_loop(0, STEPS, load, 0)
 
-    pl.semaphore_wait(barrier, len(greeted))
+    pl.semaphore_wait(barrier, RED + count(key < own_key for key in keys))
     a_remote = pltpu.make_async_remote_copy(
         src_ref=abuf.at[:, core],
         dst_ref=abuf.at[:, core],
@@ -67,8 +84,20 @@
     )
     a_copy.wait()
     a_remote.start()
-    for peer in z_peers[2:]:
-        pl.semaphore_signal(z_sem, inc=1, device_id=peer, device_id_type=MESH)
+    for other in range(NC):
+
+        @pl.when(keys[other] < own_key)
+        def _(other=other):
+            pl.semaphore_signal(
+                late_sem.at[lax.div(z, 4)], inc=1, device_id=(other * 2 + core, red), device_id_type=MESH
+            )
+
+    def all_in(half):
+        later = count(own_key < keys[t * NZ + m] for t in range(NY) for m in range(4 * half, 4 * half + 4))
+
+        @pl.when(later > 0)
+        def _():
+            pl.semaphore_wait(late_sem.at[half], later)
 
     vir_copy.wait()
     cd_copy.wait()
@@ -187,20 +216,29 @@
 
         return carry
 
+    last = (y >= 2) & (z >= 4)
+
     def step(g, carry):
-        @pl.when(g == 3)
+        @pl.when(last & (g == LAG))
         def _():
-            pl.semaphore_wait(z_sem, 2)
-            for peer in y_peers:
-                pl.semaphore_signal(late_sem, inc=1, device_id=peer, device_id_type=MESH)
+            all_in(0)
+
+        @pl.when(last & (g >= LAG))
+        def _():
+            exchange(g - LAG, 0)
 
         multiply(g)
         return carry
 
     lax.fori_loop(0, STEPS, step, 0)
 
-    pl.semaphore_wait(late_sem, NY - 1)
-    lax.fori_loop(0, STEPS, exchange, 0)
+    @pl.when(jnp.logical_not(last))
+    def _():
+        all_in(0)
+
+    lax.fori_loop(jnp.where(last, STEPS - LAG, 0), STEPS // 2, exchange, 0)
+    all_in(1)
+    lax.fori_loop(STEPS // 2, STEPS, exchange, 0)
 
     jj_irrep = jnp.zeros((16, 128), jnp.int32)
     for j in range(16):
@@ -265,8 +303,7 @@
             pltpu.VMEM((NZ, NY, 4, 128), jnp.float32),
             pltpu.VMEM((NZ, 2, 8, 128), jnp.float32),
             pltpu.VMEM((NY, NZ, 32, 128), jnp.bfloat16),
-            pltpu.SemaphoreType.REGULAR,
-            pltpu.SemaphoreType.REGULAR,
+            pltpu.SemaphoreType.REGULAR((2,)),
             pltpu.SemaphoreType.DMA((3,)),
             pltpu.SemaphoreType.DMA((STEPS,)),
             pltpu.SemaphoreType.DMA,

time: 23.9 us -> 24.3 us (1.017)
  the two profiles are of different devices: /device:TPU:1 before, /device:TPU:224 now
where the time goes in v6:
time: 24.3 us
  Pallas kernels  23.5 us (97%)
  local copies, waits for them, and re-layouts  0.71 us (3%)
    pallas_call x1, Pallas kernels, local(): pl.pallas_call(kernel, out_shape=jax.ShapeDtypeStruct((NY, NZ, 32, 128),...  23.5 us
    unnamed x1, local copies, waits for them, and re-layouts  0.71 us

profile of v6, /device:TPU:224, one launch (start us, length us, event | category | flops | bytes accessed | tf_op | source)
XLA Modules:
  0.0 24.3 jit_solution(2623771029399520203)
XLA Ops:
  0.0 23.5 %ladder.1 = bf16[4,8,32,128]{3,2,1,0:T(8,128)(2,1)S(1)} custom-call(bf16[4,16,2048]{2,1,0:T(8,128)(2,1)} %bitcast.4, bf16[2048,8192]{1,0:T(8,128)(2,1)} %v_hbm.1, s32[64]{0:T(128)} %occ_hbm.1, s32[4,128]{1,0:T(4,128)} %bitcast.5, s32[2,2048]{1,0:T(2,128)} %cd_hbm.1), custom_call_target="tpu_custom_call" | custom-call | tf_op jit(solution)/shard_map/ladder/pallas_call | solution.py:287
  23.6 0.7 %copy.7 = bf16[64,16,128]{2,1,0:T(8,128)(2,1)} copy(bf16[64,16,128]{2,1,0:T(8,128)(2,1)S(1)} %bitcast.3) | data formatting | bytes 524288

commit v7 on v6

--- a/solution.py
+++ b/solution.py
@@ -12,8 +12,12 @@
 RED = 4
 QG = NY
 STEPS = NC // QG
-LAG = 5
 MESH = pl.DeviceIdType.MESH
+
+
+def line_at(g):
+    half = lax.div(g + 1, 2)
+    return lax.rem(half * (1 - 2 * lax.rem(g + 1, 2)) + NZ, NZ)
 
 
 def start_key(of_y, of_z, chip):
@@ -63,15 +67,19 @@
         def _(other=other):
             pl.semaphore_signal(barrier, inc=1, device_id=(other * 2 + core, red), device_id_type=MESH)
 
-    def load(g, carry):
-        for t in range(QG):
-            start = pl.multiple_of(((t * NZ + g) * 2 + core) * 128, 128)
-            pltpu.make_async_copy(
-                v_hbm.at[:, pl.ds(start, 128)], vbuf.at[g, :, pl.ds(128 * t, 128)], v_sem.at[g]
-            ).start()
-        return carry
-
-    lax.fori_loop(0, STEPS, load, 0)
+    def load(m, carry):
+        for half in range(2):
+            of_z = line_at(2 * m + half)
+            for t in range(QG):
+                start = pl.multiple_of(((t * NZ + of_z) * 2 + core) * 128, 128)
+                pltpu.make_async_copy(
+                    v_hbm.at[:, pl.ds(start, 128)],
+                    vbuf.at[m, :, pl.ds(128 * (QG * half + t), 128)],
+                    v_sem.at[m],
+                ).start()
+        return carry
+
+    lax.fori_loop(0, STEPS // 2, load, 0)
 
     pl.semaphore_wait(barrier, RED + count(key < own_key for key in keys))
     a_remote = pltpu.make_async_remote_copy(
@@ -88,16 +96,7 @@
 
         @pl.when(keys[other] < own_key)
         def _(other=other):
-            pl.semaphore_signal(
-                late_sem.at[lax.div(z, 4)], inc=1, device_id=(other * 2 + core, red), device_id_type=MESH
-            )
-
-    def all_in(half):
-        later = count(own_key < keys[t * NZ + m] for t in range(NY) for m in range(4 * half, 4 * half + 4))
-
-        @pl.when(later > 0)
-        def _():
-            pl.semaphore_wait(late_sem.at[half], later)
+            pl.semaphore_signal(late_sem, inc=1, device_id=(other * 2 + core, red), device_id_type=MESH)
 
     vir_copy.wait()
     cd_copy.wait()
@@ -162,29 +161,32 @@
             device_id_type=MESH,
         )
 
-    def multiply(g):
-        pltpu.make_async_copy(vbuf.at[g], vbuf.at[g], v_sem.at[g]).wait()
-        product = jnp.dot(lhs[...], vbuf[g], preferred_element_type=jnp.float32)
-        split = []
-        for t in range(QG):
-            turned = jnp.transpose(product[:, 128 * t : 128 * (t + 1)])
-            kept = turned[0:16]
-            for h in range(1, 8):
-                kept = jnp.where(h_lane == h, turned[16 * h : 16 * (h + 1)], kept)
-            first, second = kept[0:8], kept[8:16]
-            split.append((
-                jnp.where(low64, first, pltpu.roll(second, 64, 1)),
-                jnp.where(low64, pltpu.roll(first, 64, 1), second),
-            ))
-        for n in range(QG // 2):
-            for b in range(2):
-                one, two = split[2 * n][b], split[2 * n + 1][b]
-                upper = jnp.where(low4, one, pltpu.roll(two, 4, 0))
-                lower = jnp.where(low4, pltpu.roll(one, 4, 0), two)
-                xbuf[g, 2 * b, n] = jnp.where(low32, upper, pltpu.roll(lower, 32, 1))
-                xbuf[g, 2 * b + 1, n] = jnp.where(low32, pltpu.roll(upper, 96, 1), lower)
-        for k in range(1, RED):
-            red_copy(g, k).start()
+    def multiply(m, carry):
+        pltpu.make_async_copy(vbuf.at[m], vbuf.at[m], v_sem.at[m]).wait()
+        product = jnp.dot(lhs[...], vbuf[m], preferred_element_type=jnp.float32)
+        for half in range(2):
+            g = 2 * m + half
+            split = []
+            for t in range(QG * half, QG * (half + 1)):
+                turned = jnp.transpose(product[:, 128 * t : 128 * (t + 1)])
+                kept = turned[0:16]
+                for h in range(1, 8):
+                    kept = jnp.where(h_lane == h, turned[16 * h : 16 * (h + 1)], kept)
+                first, second = kept[0:8], kept[8:16]
+                split.append((
+                    jnp.where(low64, first, pltpu.roll(second, 64, 1)),
+                    jnp.where(low64, pltpu.roll(first, 64, 1), second),
+                ))
+            for n in range(QG // 2):
+                for b in range(2):
+                    one, two = split[2 * n][b], split[2 * n + 1][b]
+                    upper = jnp.where(low4, one, pltpu.roll(two, 4, 0))
+                    lower = jnp.where(low4, pltpu.roll(one, 4, 0), two)
+                    xbuf[g, 2 * b, n] = jnp.where(low32, upper, pltpu.roll(lower, 32, 1))
+                    xbuf[g, 2 * b + 1, n] = jnp.where(low32, pltpu.roll(upper, 96, 1), lower)
+            for k in range(1, RED):
+                red_copy(g, k).start()
+        return carry
 
     def exchange(g, carry):
         for k in range(1, RED):
@@ -196,12 +198,13 @@
         for n in range(QG // 2):
             sbuf[g, 2 * n] = total[n, 0:4]
             sbuf[g, 2 * n + 1] = total[n, 4:8]
+        of_z = line_at(g)
         for t in range(QG):
-            own = (y == t) & (z == g)
+            own = (y == t) & (z == of_z)
 
             @pl.when(own)
             def _():
-                pltpu.make_async_copy(sbuf.at[g, t], fbuf.at[g, t], aa_recv.at[g]).start()
+                pltpu.make_async_copy(sbuf.at[g, t], fbuf.at[of_z, t], aa_recv.at[of_z]).start()
 
             @pl.when(jnp.logical_not(own))
             def _():
@@ -210,35 +213,21 @@
                     dst_ref=fbuf.at[z, y],
                     send_sem=aa_send,
                     recv_sem=aa_recv.at[z],
-                    device_id=((t * NZ + g) * 2 + core, red),
+                    device_id=((t * NZ + of_z) * 2 + core, red),
                     device_id_type=MESH,
                 ).start()
 
         return carry
 
-    last = (y >= 2) & (z >= 4)
-
-    def step(g, carry):
-        @pl.when(last & (g == LAG))
-        def _():
-            all_in(0)
-
-        @pl.when(last & (g >= LAG))
-        def _():
-            exchange(g - LAG, 0)
-
-        multiply(g)
-        return carry
-
-    lax.fori_loop(0, STEPS, step, 0)
-
-    @pl.when(jnp.logical_not(last))
+    lax.fori_loop(0, STEPS // 2, multiply, 0)
+
+    later = count(own_key < key for key in keys)
+
+    @pl.when(later > 0)
     def _():
-        all_in(0)
-
-    lax.fori_loop(jnp.where(last, STEPS - LAG, 0), STEPS // 2, exchange, 0)
-    all_in(1)
-    lax.fori_loop(STEPS // 2, STEPS, exchange, 0)
+        pl.semaphore_wait(late_sem, later)
+
+    lax.fori_loop(0, STEPS, exchange, 0)
 
     jj_irrep = jnp.zeros((16, 128), jnp.int32)
     for j in range(16):
@@ -290,7 +279,7 @@
         in_specs=[hbm] * 5,
         out_specs=hbm,
         scratch_shapes=[
-            pltpu.VMEM((STEPS, depth, QG * 128), jnp.bfloat16),
+            pltpu.VMEM((STEPS // 2, depth, 2 * QG * 128), jnp.bfloat16),
             pltpu.VMEM((RED, 2, 16, depth), jnp.bfloat16),
             pltpu.VMEM((128, depth), jnp.bfloat16),
             pltpu.VMEM((2, depth), jnp.int32),
@@ -303,9 +292,9 @@
             pltpu.VMEM((NZ, NY, 4, 128), jnp.float32),
             pltpu.VMEM((NZ, 2, 8, 128), jnp.float32),
             pltpu.VMEM((NY, NZ, 32, 128), jnp.bfloat16),
-            pltpu.SemaphoreType.REGULAR((2,)),
+            pltpu.SemaphoreType.REGULAR,
             pltpu.SemaphoreType.DMA((3,)),
-            pltpu.SemaphoreType.DMA((STEPS,)),
+            pltpu.SemaphoreType.DMA((STEPS // 2,)),
             pltpu.SemaphoreType.DMA,
             pltpu.SemaphoreType.DMA,
             pltpu.SemaphoreType.DMA,

time: 24.3 us -> 22.7 us (0.934)
  the two profiles are of different devices: /device:TPU:224 before, /device:TPU:1 now
where the time goes in v7:
time: 22.7 us; the launch traced here: 22.6 us
  Pallas kernels  21.9 us (96%)
  local copies, waits for them, and re-layouts  0.71 us (3%)
    pallas_call x1, Pallas kernels, local(): pl.pallas_call(kernel, out_shape=jax.ShapeDtypeStruct((NY, NZ, 32, 128),...  21.9 us
    unnamed x1, local copies, waits for them, and re-layouts  0.71 us

profile of v7, /device:TPU:1, one launch (start us, length us, event | category | flops | bytes accessed | tf_op | source)
XLA Modules:
  0.0 22.6 jit_solution(7622028747558899740)
XLA Ops:
  0.0 21.9 %ladder.1 = bf16[4,8,32,128]{3,2,1,0:T(8,128)(2,1)S(1)} custom-call(bf16[4,16,2048]{2,1,0:T(8,128)(2,1)} %bitcast.4, bf16[2048,8192]{1,0:T(8,128)(2,1)} %v_hbm.1, s32[64]{0:T(128)} %occ_hbm.1, s32[4,128]{1,0:T(4,128)} %bitcast.5, s32[2,2048]{1,0:T(2,128)} %cd_hbm.1), custom_call_target="tpu_custom_call" | custom-call | tf_op jit(solution)/shard_map/ladder/pallas_call | solution.py:276
  21.9 0.7 %copy.7 = bf16[64,16,128]{2,1,0:T(8,128)(2,1)} copy(bf16[64,16,128]{2,1,0:T(8,128)(2,1)S(1)} %bitcast.3) | data formatting | bytes 524288

commit v8 on v7

--- a/solution.py
+++ b/solution.py
@@ -12,16 +12,15 @@
 RED = 4
 QG = NY
 STEPS = NC // QG
+Y_KEYS = (0, 7, 15, 21)
+Z_KEYS = (0, 6, 12, 17, 20, 23, 26, 29)
+START_KEYS = tuple((Y_KEYS[n // NZ] + Z_KEYS[n % NZ]) * NC + n for n in range(NC))
 MESH = pl.DeviceIdType.MESH
 
 
 def line_at(g):
     half = lax.div(g + 1, 2)
     return lax.rem(half * (1 - 2 * lax.rem(g + 1, 2)) + NZ, NZ)
-
-
-def start_key(of_y, of_z, chip):
-    return (of_y + of_z) * NC + chip
 
 
 def kernel(
@@ -49,12 +48,8 @@
     barrier = pltpu.get_barrier_semaphore()
     partner = (chip * 2 + 1 - core, red)
     red_peers = [(pair, lax.rem(red + k, RED)) for k in range(1, RED)]
-    own_key = start_key(jnp.where(y < 2, 11 * y, 3 * y + 15), jnp.where(z < 4, 9 * z, z + 27), chip)
-    keys = [
-        start_key(11 * t if t < 2 else 3 * t + 15, 9 * m if m < 4 else m + 27, t * NZ + m)
-        for t in range(NY)
-        for m in range(NZ)
-    ]
+    own_key = sum(jnp.where(chip == n, key, 0) for n, key in enumerate(START_KEYS))
+    keys = START_KEYS
 
     def count(conditions):
         return sum(jnp.where(condition, 1, 0) for condition in conditions)
@@ -144,7 +139,7 @@
         lhs[:, at] = jnp.where(keep, block, 0.0).astype(jnp.bfloat16)
         return carry
 
-    lax.fori_loop(0, depth // width, mask, 0)
+    lax.fori_loop(0, depth // width, mask, 0, unroll=True)
 
     low64 = lane8 < 64
     low32 = (lane8 & 32) == 0
@@ -261,13 +256,12 @@
     lax.fori_loop(0, NZ, arrive, 0)
     for n in range(NZ):
         finish(n)
-    out_copy = pltpu.make_async_copy(obuf, o_hbm, out_sem)
-    out_copy.start()
+        pltpu.make_async_copy(obuf.at[:, n], o_hbm.at[:, n], out_sem).start()
     sent = xbuf.at[:, pl.ds(0, RED - 1)]
     pltpu.make_async_copy(sent, sent, rs_send).wait()
     all_sent = sbuf.reshape(NC, 4, 128).at[pl.ds(0, NC - 1)]
     pltpu.make_async_copy(all_sent, all_sent, aa_send).wait()
-    out_copy.wait()
+    pltpu.make_async_copy(obuf, o_hbm, out_sem).wait()
 
 
 def local(amplitudes, integrals, occ_irrep, vir_irrep, cd_orbitals, ab_orbitals):

time: 22.7 us -> 24.1 us (1.062)
  Pallas kernels: 21.9 us -> 23.3 us
    pallas_call x1, Pallas kernels: 21.9 us -> 23.3 us  [local(): pl.pallas_call(kernel, out_shape=jax.ShapeDtypeStruct((NY, NZ, 32, 128),...]
where the time goes in v8:
time: 24.1 us; the launch traced here: 24 us
  Pallas kernels  23.3 us (97%)
  local copies, waits for them, and re-layouts  0.71 us (3%)
    pallas_call x1, Pallas kernels, local(): pl.pallas_call(kernel, out_shape=jax.ShapeDtypeStruct((NY, NZ, 32, 128),...  23.3 us
    unnamed x1, local copies, waits for them, and re-layouts  0.71 us

profile of v8, /device:TPU:1, one launch (start us, length us, event | category | flops | bytes accessed | tf_op | source)
XLA Modules:
  0.0 24.0 jit_solution(3765920217169614374)
XLA Ops:
  0.0 23.3 %ladder.1 = bf16[4,8,32,128]{3,2,1,0:T(8,128)(2,1)S(1)} custom-call(bf16[4,16,2048]{2,1,0:T(8,128)(2,1)} %bitcast.4, bf16[2048,8192]{1,0:T(8,128)(2,1)} %v_hbm.1, s32[64]{0:T(128)} %occ_hbm.1, s32[4,128]{1,0:T(4,128)} %bitcast.5, s32[2,2048]{1,0:T(2,128)} %cd_hbm.1), custom_call_target="tpu_custom_call" | custom-call | tf_op jit(solution)/shard_map/ladder/pallas_call | solution.py:270
  23.3 0.7 %copy.7 = bf16[64,16,128]{2,1,0:T(8,128)(2,1)} copy(bf16[64,16,128]{2,1,0:T(8,128)(2,1)S(1)} %bitcast.3) | data formatting | bytes 524288

commit v9 on v7

--- a/solution.py
+++ b/solution.py
@@ -80,23 +80,6 @@
         return carry
 
     lax.fori_loop(0, STEPS // 2, load, 0)
-
-    pl.semaphore_wait(barrier, RED + count(key < own_key for key in keys))
-    a_remote = pltpu.make_async_remote_copy(
-        src_ref=abuf.at[:, core],
-        dst_ref=abuf.at[:, core],
-        send_sem=a_send,
-        recv_sem=a_recv,
-        device_id=partner,
-        device_id_type=MESH,
-    )
-    a_copy.wait()
-    a_remote.start()
-    for other in range(NC):
-
-        @pl.when(keys[other] < own_key)
-        def _(other=other):
-            pl.semaphore_signal(late_sem, inc=1, device_id=(other * 2 + core, red), device_id_type=MESH)
 
     vir_copy.wait()
     cd_copy.wait()
@@ -134,6 +117,23 @@
     h_lane = i_irrep ^ j_irrep
     h_rows = jnp.transpose(jnp.broadcast_to(h_lane[0:1].astype(jnp.float32), (128, 128)))
     h_rows = h_rows[:, 0:1].astype(jnp.int32)
+
+    pl.semaphore_wait(barrier, RED + count(key < own_key for key in keys))
+    a_remote = pltpu.make_async_remote_copy(
+        src_ref=abuf.at[:, core],
+        dst_ref=abuf.at[:, core],
+        send_sem=a_send,
+        recv_sem=a_recv,
+        device_id=partner,
+        device_id_type=MESH,
+    )
+    a_copy.wait()
+    a_remote.start()
+    for other in range(NC):
+
+        @pl.when(keys[other] < own_key)
+        def _(other=other):
+            pl.semaphore_signal(late_sem, inc=1, device_id=(other * 2 + core, red), device_id_type=MESH)
 
     a_remote.wait()
 

time: 22.7 us -> 22.7 us (level)
  no operation moved by 1% of the time
where the time goes in v9:
time: 22.7 us; the launch traced here: 22.6 us
  Pallas kernels  21.9 us (96%)
  local copies, waits for them, and re-layouts  0.71 us (3%)
    pallas_call x1, Pallas kernels, local(): pl.pallas_call(kernel, out_shape=jax.ShapeDtypeStruct((NY, NZ, 32, 128),...  21.9 us
    unnamed x1, local copies, waits for them, and re-layouts  0.71 us

profile of v9, /device:TPU:1, one launch (start us, length us, event | category | flops | bytes accessed | tf_op | source)
XLA Modules:
  0.0 22.6 jit_solution(17304500333299519277)
XLA Ops:
  0.0 21.9 %ladder.1 = bf16[4,8,32,128]{3,2,1,0:T(8,128)(2,1)S(1)} custom-call(bf16[4,16,2048]{2,1,0:T(8,128)(2,1)} %bitcast.4, bf16[2048,8192]{1,0:T(8,128)(2,1)} %v_hbm.1, s32[64]{0:T(128)} %occ_hbm.1, s32[4,128]{1,0:T(4,128)} %bitcast.5, s32[2,2048]{1,0:T(2,128)} %cd_hbm.1), custom_call_target="tpu_custom_call" | custom-call | tf_op jit(solution)/shard_map/ladder/pallas_call | solution.py:276
  21.9 0.7 %copy.7 = bf16[64,16,128]{2,1,0:T(8,128)(2,1)} copy(bf16[64,16,128]{2,1,0:T(8,128)(2,1)S(1)} %bitcast.3) | data formatting | bytes 524288
